TPU v7x, 32 devices: a whole 2x2x4 slice. The times are simulated.
32 devices in a mesh: groups: 2 (over x), seq: 16 (over z, y, core).
Axes of the slice: x: 2, y: 2, z: 4, core: 2. Of those that a mesh axis runs over, the one named last changes fastest.
Arguments:
- queries: bfloat16 [12288, 2240], P(('groups', 'seq')), parts along dimension 0, may hold values from -6 to 6
- key_rows: bfloat16 [12288, 2240], P(('groups', 'seq')), parts along dimension 0, may hold values from -6 to 6
- value_rows: bfloat16 [12288, 2240], P(('groups', 'seq')), parts along dimension 0, may hold values from -6 to 6
- frame_len: int32 [32, 2], P(('groups', 'seq')), parts along dimension 0, may hold values from 1 to 240, 384 in all within a row
- log_decay: float32 [32, 2, 20], P(('groups', 'seq')), parts along dimension 0, may hold values from -6 to 0
- timestep: int32 [32], P(('groups', 'seq')), parts along dimension 0, may hold values from 0 to 49
- conv_kernel: float32 [4, 2240], replicated, may hold values from -3 to 3
- norm_gain: float32 [2240], replicated, may hold values from 0.1 to 1.9
- mod_table: float32 [50, 2240], replicated, may hold values from -3 to 3
- out_grad: bfloat16 [12288, 2240], P(('groups', 'seq')), parts along dimension 0, may hold values from -6 to 6
Outputs:
- grad_queries: bfloat16 [12288, 2240], P(('groups', 'seq')), parts along dimension 0
- grad_keys: bfloat16 [12288, 2240], P(('groups', 'seq')), parts along dimension 0
- grad_values: bfloat16 [12288, 2240], P(('groups', 'seq')), parts along dimension 0
- grad_kernel: float32 [8, 2240], P('groups'), parts along dimension 0
- grad_gain: float32 [4480], P('groups'), parts along dimension 0
- grad_table: float32 [100, 2240], P('groups'), parts along dimension 0
There are 2 independent parts, one for each index of `groups`. A program takes and returns all parts, laid end to end along the dimension named above; an argument that names none is the same for every part. Nothing has to cross between parts.
Inputs may be any that keep to these rules, and one draw needn't show every extreme that they name: `frame_len`: the 2 frames of each block hold 384 tokens together, and in every block the longest frame has at most 240 tokens.
All inputs are finite; a program needn't handle non-finite values.
Results may differ from a plain program's by a relative error of at most 0.0058.
Values may be sent and summed in bfloat16 or wider, within the bound.
A program may use at most 384 MiB of HBM per device.

v0:
```python
import jax
import jax.numpy as jnp
from jax import lax
from jax.sharding import PartitionSpec as P

EPSILON = 1e-06


def carried_in(part, axis, combine, identity, reverse):
    count = lax.axis_size(axis)
    place = lax.axis_index(axis)
    ahead = count - 1 - place if reverse else place
    gathered = jax.tree.map(lambda a: lax.all_gather(a, axis), part)
    state = jax.tree.map(lambda a, e: jnp.zeros_like(a) + jnp.asarray(e, a.dtype), part, identity)

    def one(lap, state):
        source = count - 1 - lap if reverse else lap
        return combine(
            state, jax.tree.map(lambda a: lax.dynamic_index_in_dim(a, source, 0, False), gathered)
        )

    return lax.fori_loop(0, ahead, one, state)


def passed_along(value, axis, steps):
    count = lax.axis_size(axis)
    leading, last = (max(0, -steps), min(count, count - steps))
    return lax.ppermute(value, axis, [(source, source + steps) for source in range(leading, last)])


def frame_layout(lengths, decays, count):
    bounds = jnp.cumsum(lengths)
    position = jnp.arange(count, dtype=jnp.int32)
    frame_id = jnp.sum((position[:, None] >= bounds[None, :]).astype(jnp.int32), axis=1)
    frame_cum = jnp.cumsum(decays, axis=0)
    frame_numbers = jnp.arange(lengths.shape[0], dtype=jnp.int32)
    selector = (frame_id[:, None] == frame_numbers[None, :]).astype(jnp.float32)
    token_decay = jnp.sum(selector[:, :, None] * frame_cum[None, :, :], axis=1)
    return (frame_id, token_decay, frame_cum[-1])


def decay_weights(frame_id, token_decay):
    allowed = (frame_id[:, None] >= frame_id[None, :])[None, :, :]
    head_major = token_decay.T
    spread = head_major[:, :, None] - head_major[:, None, :]
    return jnp.where(allowed, jnp.exp(jnp.where(allowed, spread, 0.0)), 0.0)


def causal_conv(padded, kernel, count):
    tap_count = kernel.shape[0]
    computed_output = jnp.zeros((count, kernel.shape[1]), jnp.float32)
    for offset in range(tap_count):
        computed_output = (
            computed_output
            + kernel[offset] * padded[tap_count - 1 - offset : tap_count - 1 - offset + count]
        )
    return computed_output


def conv_back(padded_grad, kernel, count):
    computed_output = jnp.zeros((count, kernel.shape[1]), jnp.float32)
    for offset in range(kernel.shape[0]):
        computed_output = computed_output + kernel[offset] * padded_grad[offset : offset + count]
    return computed_output


def combine_maps(earlier, later):
    return (earlier[0] * later[0], later[0][:, None, None] * earlier[1] + later[1])


def carried(factor, local_state, reverse):
    identity = (jnp.ones_like(factor), jnp.zeros_like(local_state))
    return carried_in((factor, local_state), "seq", combine_maps, identity, reverse)[1]


def body(
    queries,
    key_rows,
    value_rows,
    frame_len,
    log_decay,
    timestep,
    conv_kernel,
    norm_gain,
    mod_table,
    out_grad,
):
    exact = lax.Precision.HIGHEST
    row_count, channels = queries.shape
    head_count = log_decay.shape[2]
    head_dim = channels // head_count
    score_scale = head_dim ** (-0.5)
    tap_count = conv_kernel.shape[0]
    block_count = lax.axis_size("seq")
    frame_id, token_decay, block_decay = frame_layout(frame_len[0], log_decay[0], row_count)
    previous = passed_along(value_rows[row_count - (tap_count - 1) :], "seq", 1)
    padded = jnp.concatenate([previous, value_rows], axis=0).astype(jnp.float32)
    conv_values = causal_conv(padded, conv_kernel, row_count).astype(jnp.bfloat16)
    query_heads = queries.reshape(row_count, head_count, head_dim)
    key_heads = key_rows.reshape(row_count, head_count, head_dim)
    value_heads = conv_values.reshape(row_count, head_count, head_dim)
    value_float = value_heads.astype(jnp.float32)
    into_end = jnp.exp(block_decay[None, :] - token_decay)
    from_start = jnp.exp(token_decay)
    block_factor = jnp.exp(block_decay)
    scaled_keys = key_heads.astype(jnp.float32) * into_end[:, :, None]
    local_state = jnp.einsum("thd,the->hde", scaled_keys, value_float, precision=exact)
    state_in = carried(block_factor, local_state, False)
    weights_mask = decay_weights(frame_id, token_decay)
    scores = jnp.einsum("thd,shd->hts", query_heads, key_heads, preferred_element_type=jnp.float32)
    attn_weights = (scores * weights_mask * score_scale).astype(jnp.bfloat16)
    numerator = jnp.einsum(
        "hts,shd->thd", attn_weights, value_heads, preferred_element_type=jnp.float32
    )
    scaled_queries = query_heads.astype(jnp.float32) * (score_scale * from_start)[:, :, None]
    numerator = numerator + jnp.einsum("thd,hde->the", scaled_queries, state_in, precision=exact)
    inv_rms = lax.rsqrt(jnp.mean(numerator * numerator, axis=2, keepdims=True) + EPSILON)
    normed = numerator * inv_rms
    selector = (timestep[0] == jnp.arange(mod_table.shape[0], dtype=jnp.int32)).astype(jnp.float32)
    mod_row = jnp.sum(selector[:, None] * mod_table, axis=0)
    upstream = out_grad.astype(jnp.float32).reshape(row_count, head_count, head_dim)
    normed_grad = upstream * (norm_gain * (1.0 + mod_row)).reshape(head_count, head_dim)
    numer_grad = inv_rms * (
        normed_grad - normed * jnp.mean(normed_grad * normed, axis=2, keepdims=True)
    )
    grad_rounded = numer_grad.astype(jnp.bfloat16)
    score_grad = jnp.einsum(
        "thd,shd->hts", grad_rounded, value_heads, preferred_element_type=jnp.float32
    )
    score_grad = (score_grad * weights_mask * score_scale).astype(jnp.bfloat16)
    adjoint_local = jnp.einsum("thd,the->hde", scaled_queries, numer_grad, precision=exact)
    adjoint = carried(block_factor, adjoint_local, True)
    query_grad = jnp.einsum(
        "hts,shd->thd", score_grad, key_heads, preferred_element_type=jnp.float32
    )
    query_grad = query_grad + (score_scale * from_start)[:, :, None] * jnp.einsum(
        "the,hde->thd", numer_grad, state_in, precision=exact
    )
    key_grad = jnp.einsum(
        "hts,thd->shd", score_grad, query_heads, preferred_element_type=jnp.float32
    )
    key_grad = key_grad + into_end[:, :, None] * jnp.einsum(
        "the,hde->thd", value_float, adjoint, precision=exact
    )
    value_grad = jnp.einsum(
        "hts,thd->shd", attn_weights, grad_rounded, preferred_element_type=jnp.float32
    )
    value_grad = value_grad + jnp.einsum("thd,hde->the", scaled_keys, adjoint, precision=exact)
    conv_grad = value_grad.reshape(row_count, channels)
    following = passed_along(conv_grad[: tap_count - 1], "seq", -1)
    padded_grad = jnp.concatenate([conv_grad, following], axis=0)
    input_grad = conv_back(padded_grad, conv_kernel, row_count)
    kernel_terms = jnp.stack(
        [
            jnp.sum(
                conv_grad * padded[tap_count - 1 - offset : tap_count - 1 - offset + row_count],
                axis=0,
            )
            for offset in range(tap_count)
        ],
        axis=0,
    )
    block_terms = jnp.sum((upstream * normed).reshape(row_count, channels), axis=0)
    gain_terms = block_terms * (1.0 + mod_row)
    table_row = block_terms * norm_gain
    table_local = selector[:, None] * table_row[None, :]
    gain_sum, kernel_sum, table_sum = lax.psum((gain_terms, kernel_terms, table_local), "seq")
    return (
        query_grad.reshape(row_count, channels).astype(jnp.bfloat16),
        key_grad.reshape(row_count, channels).astype(jnp.bfloat16),
        input_grad.astype(jnp.bfloat16),
        kernel_sum / block_count,
        gain_sum / block_count,
        table_sum / block_count,
    )


def solution(mesh):
    in_specs = (
        P(("groups", "seq"), None),
        P(("groups", "seq"), None),
        P(("groups", "seq"), None),
        P(("groups", "seq"), None),
        P(("groups", "seq"), None, None),
        P(("groups", "seq")),
        P(),
        P(),
        P(),
        P(("groups", "seq"), None),
    )
    out_specs = (
        P(("groups", "seq"), None),
        P(("groups", "seq"), None),
        P(("groups", "seq"), None),
        P("groups", None),
        P("groups"),
        P("groups", None),
    )
    return jax.shard_map(body, mesh=mesh, in_specs=in_specs, out_specs=out_specs, check_vma=False)
```

profile of v0, /device:TPU:0, one launch (start us, length us, event | category | flops | bytes accessed | tf_op | source)
XLA Modules:
  0.0 512.1 jit_solution(10297591328339129752)
XLA Ops:
  16.3 4.3 add_convert_fusion
  21.8 3.3 fusion.22
  26.6 22.6 %all-gather.2 = f32[16,1,20]{2,1,0:T(1,128)S(1)} all-gather(f32[1,1,20]{2,1,0:T(1,128)S(1)} %copy-done.36), channel_id=1, replica_groups=mesh['groups'=2,'seq'=16] {'seq'}, dimensions={0}, use_global_device_ids=true | all-gather | bytes 1360 | tf_op jit(solution)/shard_map/all_gather | solution.py:13
  49.3 7.4 %multiply_convert_fusion.1 = bf16[20,384,384]{2,1,0:T(8,128)(2,1)} fusion(f32[20,384]{1,0:T(8,128)S(1)} %bitcast.115, pred[384,384]{1,0:T(8,128)(4,1)S(1)} %broadcast_compare_fusion, bf16[384,20,112]{0,2,1:T(8,128)(2,1)S(1)} %bitcast.101, bf16[384,20,112]{0,2,1:T(8,128)(2,1)} %bitcast.106), kind=kOutput, calls=%fused_computation.5 | convolution fusion | flops 678297600 | bytes 9517056 | tf_op jit(solution)/shard_map/thd,shd->hts/dot_general | solution.py:110
  56.7 67.6 %all-gather.6.cloned.1.call-done = f32[320,112,112]{2,1,0:T(8,128)} async-done(((f32[20,112,112]{2,1,0:T(8,128)}), f32[320,112,112]{2,1,0:T(8,128)}) %all-gather.6.cloned.1.call-update) | async-done | bytes 16056336 | tf_op jit(solution)/shard_map/all_gather | solution.py:13
  125.7 3.3 fusion.20
  129.0 4.8 fusion.18
  139.8 8.0 %fusion.19 = f32[20,112,112]{2,1,0:T(8,128)} fusion(bf16[384,20,112]{0,2,1:T(8,128)(2,1)} %bitcast.100, f32[384,20]{0,1:T(8,128)S(1)} %get-tuple-element.169, bf16[384,20,112]{0,2,1:T(8,128)(2,1)} %bitcast.91, f32[20,112,384]{2,1,0:T(8,128)S(1)} %get-tuple-element.176, f32[384,20]{0,1:T(8,128)S(1)} %broadcast_multiply_fusion.3, f32[20,112]{1,0:T(8,128)} %copy-done.19, ...), kind=kOutput, calls=%fused_computation.42 | convolution fusion | flops 1162936320 | bytes 7985920 | tf_op jit(solution)/shard_map/thd,the->hde/dot_general | solution.py:131
  147.8 7.3 %multiply_convert_fusion = bf16[20,384,384]{2,1,0:T(8,128)(2,1)S(1)} fusion(f32[20,384]{1,0:T(8,128)} %bitcast.116, pred[384,384]{1,0:T(8,128)(4,1)} %copy-done.23, bf16[384,20,112]{0,2,1:T(8,128)(2,1)} %bitcast.97, bf16[384,20,112]{0,2,1:T(8,128)(2,1)} %bitcast.92, f32[20,112,384]{2,1,0:T(8,128)S(1)} %get-tuple-element.176, ...), kind=kOutput, calls=%fused_computation.4 | convolution fusion | flops 684318720 | bytes 13028096 | tf_op jit(solution)/shard_map/thd,shd->hts/dot_general | solution.py:127
  155.1 3.2 fusion.36
  160.3 5.0 fusion.17
  165.3 87.6 %all-reduce.3.cloned.1.call-done = f32[50,2240]{1,0:T(8,128)} async-done(((f32[50,2240]{1,0:T(8,128)}), f32[50,2240]{1,0:T(8,128)}) %all-reduce.3.cloned.1.call-update) | async-done | bytes 448016 | tf_op jit(solution)/shard_map/psum | solution.py:167
  254.7 97.0 %all-gather.8.cloned.1.call-done = f32[320,112,112]{2,1,0:T(8,128)} async-done(((f32[20,112,112]{2,1,0:T(8,128)}), f32[320,112,112]{2,1,0:T(8,128)}) %all-gather.8.cloned.1.call-update) | async-done | bytes 16056336 | tf_op jit(solution)/shard_map/all_gather | solution.py:13
  352.8 52.0 %while.27 = (s32[]{:T(128)}, f32[20,112,112]{2,1,0:T(8,128)}, s32[]{:T(128)}, f32[16,20]{1,0:T(8,128)}, f32[16,20,112,112]{3,2,1,0:T(8,128)}, /*index=5*/s32[]{:T(128)}, s32[]{:T(128)}, s32[]{:T(128)}, s32[]{:T(128)}) while((s32[]{:T(128)}, f32[20,112,112]{2,1,0:T(8,128)}, s32[]{:T(128)}, f32[16,20]{1,0:T(8,128)}, ...), condition=%wide.region_10.11_spmd, body=%wide.region_9.10_spmd.sunk | while | flops 501766 | bytes 3010947 | solution.py:22
  353.5 2.8 bitcast_add_fusion.5
  357.0 2.8 bitcast_add_fusion.5
  360.5 2.8 bitcast_add_fusion.5
  363.9 2.8 bitcast_add_fusion.5
  367.4 2.8 bitcast_add_fusion.5
  370.9 2.8 bitcast_add_fusion.5
  374.3 2.8 bitcast_add_fusion.5
  377.8 2.8 bitcast_add_fusion.5
  381.3 2.8 bitcast_add_fusion.5
  384.7 2.8 bitcast_add_fusion.5
  391.6 2.8 bitcast_add_fusion.5
  395.1 2.8 bitcast_add_fusion.5
  402.0 2.8 bitcast_add_fusion.5
  404.8 5.5 %fusion.21 = f32[20,112,384]{2,1,0:T(8,128)S(1)} fusion(f32[20,112,112]{2,1,0:T(8,128)} %get-tuple-element.135, bf16[384,20,112]{0,2,1:T(8,128)(2,1)} %bitcast.107, f32[384,20]{0,1:T(8,128)S(1)} %copy-done.17), kind=kOutput, calls=%fused_computation.45 | convolution fusion | flops 1157775360 | bytes 6195200 | tf_op jit(solution)/shard_map/thd,hde->the/dot_general | solution.py:148
  410.3 4.0 convolution_add_fusion
  420.3 4.8 fusion.15
  425.6 19.5 %multiply_reduce_fusion.3 = (f32[2240]{0:T(1024)S(1)}, f32[2240]{0:T(1024)S(1)}, f32[2240]{0:T(1024)S(1)}, f32[2240]{0:T(1024)S(1)}, bf16[384,2240]{0,1:T(8,128)(2,1)}) fusion(f32[384,2240]{0,1:T(8,128)} %bitcast.105, f32[387,2240]{0,1:T(8,128)} %copy-done, f32[3,2240]{0,1:T(8,128)S(1)} %copy.30, f32[2240]{0:T(1024)S(1)} %copy-done.30, ...), kind=kLoop, calls=%fused_computation.40 | loop fusion | flops 16334080 | bytes 19022080 | tf_op jit(solution)/shard_map/reduce_sum | solution.py:155
  445.2 58.7 %all-reduce = (f32[4,2240]{1,0:T(4,128)S(1)}, f32[2240]{0:T(1024)S(1)}) all-reduce(f32[4,2240]{1,0:T(4,128)S(1)} %pad_maximum_fusion.1, f32[2240]{0:T(1024)S(1)} %copy-done.34), channel_id=1, replica_groups=mesh['groups'=2,'seq'=16] {'seq'}, use_global_device_ids=true, to_apply=%region_15.16 | all-reduce | flops 11200 | bytes 89600 | tf_op jit(solution)/shard_map/psum | solution.py:167
  (140 shorter events, 46.6 us)
Async XLA Ops:
  7.2 8.0 %copy-start.15 = (bf16[384,2240]{0,1:T(8,128)(2,1)S(1)}, bf16[384,2240]{0,1:T(8,128)(2,1)}, u32[]{:S(2)}) copy-start(bf16[384,2240]{0,1:T(8,128)(2,1)} %param.16) | copy-start | bytes 5160964
  7.2 117.2 %all-gather.6.cloned.1.call-start = ((), (), s32[]{:S(2)}) async-start(), calls=%async_computation.1 | async-start | bytes 19496960 | tf_op jit(solution)/shard_map/all_gather | solution.py:13
  8.9 6.0 %collective-permute-start = (bf16[3,2240]{1,0:T(4,128)(2,1)S(1)}, bf16[3,2240]{1,0:T(4,128)(2,1)S(1)}, u32[]{:S(2)}, u32[]{:S(2)}) collective-permute-start(bf16[3,2240]{1,0:T(4,128)(2,1)S(1)} %copy.33), channel_id=1, source_target_pairs={{0,1},{1,2},{2,3},{3,4},{4,5},{5,6},{6,7},{7,8},{8,9},{9,10},{10,1... | collective-permute-start | bytes 40328 | tf_op jit(solution)/shard_map/ppermute | solution.py:28
  13.6 35.7 %copy-start.22 = (f32[384,20]{0,1:T(8,128)}, f32[384,20]{0,1:T(8,128)S(1)}, u32[]{:S(2)}) copy-start(f32[384,20]{0,1:T(8,128)S(1)} %multiply_reduce_fusion.5) | copy-start | bytes 92164
  13.7 7.0 %copy-start.16 = (f32[384,20]{0,1:T(8,128)}, f32[384,20]{0,1:T(8,128)S(1)}, u32[]{:S(2)}) copy-start(f32[384,20]{0,1:T(8,128)S(1)} %get-tuple-element.170) | copy-start | bytes 92164
  16.2 4.4 copy-start
  16.3 5.5 %copy-start.13 = (bf16[384,2240]{0,1:T(8,128)(2,1)S(1)}, bf16[384,2240]{0,1:T(8,128)(2,1)}, u32[]{:S(2)}) copy-start(bf16[384,2240]{0,1:T(8,128)(2,1)} %param.15) | copy-start | bytes 5160964
  20.6 5.2 %copy-start.18 = (f32[50,2240]{1,0:T(8,128)S(1)}, f32[50,2240]{1,0:T(8,128)}, u32[]{:S(2)}) copy-start(f32[50,2240]{1,0:T(8,128)} %param.22) | copy-start | bytes 1344004
  20.6 5.4 %copy-start.33 = (f32[2240]{0:T(1024)S(1)}, f32[2240]{0:T(1024)}, u32[]{:S(2)}) copy-start(f32[2240]{0:T(1024)} %param.21) | copy-start | bytes 26884
  20.7 5.9 %copy-start.36 = (f32[1,1,20]{2,1,0:T(1,128)S(1)}, f32[1,1,20]{2,1,0:T(1,128)}, u32[]{:S(2)}) copy-start(f32[1,1,20]{2,1,0:T(1,128)} %get-tuple-element.174) | copy-start | bytes 244
  20.7 28.7 %copy-start.10 = (bf16[384,2240]{0,1:T(8,128)(2,1)S(1)}, bf16[384,2240]{0,1:T(8,128)(2,1)}, u32[]{:S(2)}) copy-start(bf16[384,2240]{0,1:T(8,128)(2,1)} %param.14) | copy-start | bytes 5160964
  25.1 227.7 %all-reduce.3.cloned.1.call-start = ((), (), s32[]{:S(2)}) async-start(), calls=%async_computation | async-start | bytes 1032192 | tf_op jit(solution)/shard_map/psum | solution.py:167
  26.1 107.7 %copy-start.19 = (f32[20,112]{1,0:T(8,128)}, f32[20,112]{1,0:T(8,128)S(1)}, u32[]{:S(2)}) copy-start(f32[20,112]{1,0:T(8,128)S(1)} %mul.272) | copy-start | bytes 26884
  49.3 7.4 %copy-start.23 = (pred[384,384]{1,0:T(8,128)(4,1)}, pred[384,384]{1,0:T(8,128)(4,1)S(1)}, u32[]{:S(2)}) copy-start(pred[384,384]{1,0:T(8,128)(4,1)S(1)} %broadcast_compare_fusion) | copy-start | bytes 442372
  124.7 9.2 %copy-start.35 = (f32[16,20]{1,0:T(8,128)}, f32[16,20]{1,0:T(8,128)S(1)}, u32[]{:S(2)}) copy-start(f32[16,20]{1,0:T(8,128)S(1)} %get-tuple-element.308) | copy-start | bytes 3844
  124.7 4.3 copy-start.8
  129.0 4.9 copy-start.4
  139.7 212.0 %all-gather.8.cloned.1.call-start = ((), (), s32[]{:S(2)}) async-start(), calls=%async_computation.2 | async-start | bytes 19496960 | tf_op jit(solution)/shard_map/all_gather | solution.py:13
  147.8 7.3 %copy-start.11 = (bf16[384,2240]{0,1:T(8,128)(2,1)S(1)}, bf16[384,2240]{0,1:T(8,128)(2,1)}, u32[]{:S(2)}) copy-start(bf16[384,2240]{0,1:T(8,128)(2,1)} %param.14) | copy-start | bytes 5160964
  155.1 3.2 copy-start.14
  158.3 2.0 copy-start.20
  352.8 52.0 %copy-start.17 = (f32[384,20]{0,1:T(8,128)S(1)}, f32[384,20]{0,1:T(8,128)}, u32[]{:S(2)}) copy-start(f32[384,20]{0,1:T(8,128)} %copy-done.16) | copy-start | bytes 92164
  404.8 5.5 %copy-start.6 = (bf16[384,2240]{0,1:T(8,128)(2,1)S(1)}, bf16[384,2240]{0,1:T(8,128)(2,1)}, u32[]{:S(2)}) copy-start(bf16[384,2240]{0,1:T(8,128)(2,1)} %param.23) | copy-start | bytes 5160964
  404.8 5.5 %copy-start.21 = (f32[20,112]{1,0:T(8,128)S(1)}, f32[20,112]{1,0:T(8,128)}, u32[]{:S(2)}) copy-start(f32[20,112]{1,0:T(8,128)} %copy-done.19) | copy-start | bytes 26884
  414.4 5.9 %copy-start.1 = (f32[20,112,112]{2,1,0:T(8,128)S(1)}, f32[20,112,112]{2,1,0:T(8,128)}, u32[]{:S(2)}) copy-start(f32[20,112,112]{2,1,0:T(8,128)} %get-tuple-element.135) | copy-start | bytes 3010564
  414.4 5.9 %copy-start.9 = (bf16[384,2240]{0,1:T(8,128)(2,1)S(1)}, bf16[384,2240]{0,1:T(8,128)(2,1)}, u32[]{:S(2)}) copy-start(bf16[384,2240]{0,1:T(8,128)(2,1)} %copy-done.7) | copy-start | bytes 5160964
  418.8 6.7 %copy-start.26 = (f32[2240]{0:T(1024)S(1)}, f32[2240]{0:T(1024)}, u32[]{:S(2)}) copy-start(f32[2240]{0:T(1024)} %copy-done.25) | copy-start | bytes 26884
  418.8 6.7 %copy-start.28 = (f32[2240]{0:T(1024)S(1)}, f32[2240]{0:T(1024)}, u32[]{:S(2)}) copy-start(f32[2240]{0:T(1024)} %copy-done.27) | copy-start | bytes 26884
  418.8 6.7 %copy-start.30 = (f32[2240]{0:T(1024)S(1)}, f32[2240]{0:T(1024)}, u32[]{:S(2)}) copy-start(f32[2240]{0:T(1024)} %copy-done.29) | copy-start | bytes 26884
  418.8 6.7 %copy-start.32 = (f32[2240]{0:T(1024)S(1)}, f32[2240]{0:T(1024)}, u32[]{:S(2)}) copy-start(f32[2240]{0:T(1024)} %copy-done.31) | copy-start | bytes 26884
  418.8 6.3 %collective-permute-start.1 = (f32[3,2240]{1,0:T(4,128)S(1)}, f32[3,2240]{1,0:T(4,128)S(1)}, u32[]{:S(2)}, u32[]{:S(2)}) collective-permute-start(f32[3,2240]{1,0:T(4,128)S(1)} %copy.29), channel_id=1, source_target_pairs={{1,0},{2,1},{3,2},{4,3},{5,4},{6,5},{7,6},{8,7},{9,8},{10,9},{11,1... | collective-permute-start | bytes 80648 | tf_op jit(solution)/shard_map/ppermute | solution.py:28
  425.6 19.6 %copy-start.34 = (f32[2240]{0:T(1024)S(1)}, f32[2240]{0:T(1024)}, u32[]{:S(2)}) copy-start(f32[2240]{0:T(1024)} %get-tuple-element.172) | copy-start | bytes 26884
  (10 other events, 14.4 us)
Sparse Core Ops, SparseCore 0:
  25.3 99.0 all-gather.5
  139.8 112.9 all-reduce.2
  254.5 97.2 all-gather.7
where the time goes:
time: 520 us; the launch traced here: 512 us
  waiting for transfers between devices  252 us (48%)
  blocking collectives  81.3 us (16%)
  other arithmetic  76.3 us (15%)
  matrix products  58.6 us (11%)
  local copies, waits for them, and re-layouts  24.1 us (5%)
  between operations  15.5 us (3%)
    all_gather x2, waiting for transfers between devices, carried_in(): gathered = jax.tree.map(lambda a: lax.all_gather(a, axis), part)  165 us
    psum x1, waiting for transfers between devices, body(): lax.psum((gain_terms, kernel_terms, table_local), 'seq')  87.6 us
    psum x1, blocking collectives, body(): lax.psum((gain_terms, kernel_terms, table_local), 'seq')  58.7 us
    add x15, other arithmetic, combine_maps(): later[0][:, None, None] * earlier[1] + later[1]  41.7 us
    all_gather x1, blocking collectives, carried_in(): gathered = jax.tree.map(lambda a: lax.all_gather(a, axis), part)  22.6 us
    reduce_sum x1, other arithmetic, body(): jnp.sum(conv_grad * padded[tap_count - 1 - offset:tap_count - 1 - offset...  19.5 us
  transfers between devices with their start and end apart: 5, of which 3 were waited for; matrix products, arithmetic and copies ran while one was open for 8% of the time, Pallas kernels for 0%

commit v1 on v0

v1 whole, which is shorter than its diff:
```python
import functools

import jax
import jax.numpy as jnp
from jax import lax
from jax.experimental import pallas as pl
from jax.experimental.pallas import tpu as pltpu
from jax.sharding import PartitionSpec as P

EPSILON = 1e-06
MESH = pl.DeviceIdType.MESH


def scan_kernel(n, rows, head_dim, reverse, *refs):
    if reverse:
        (pieces, extra, decays, out, extra_all, inbox, outbox) = refs[:7]
    else:
        (pieces, extra, out, extra_all, inbox, outbox) = refs[:6]
        decays = extra_all
    (in_send, in_recv, ex_send, ex_recv, out_send, out_recv) = refs[-6:]
    me = lax.axis_index("seq")
    group = lax.axis_index("groups")

    def where(peer):
        return (group, peer)

    def piece_copy(peer, slot):
        return pltpu.make_async_remote_copy(
            src_ref=pieces.at[peer], dst_ref=inbox.at[slot],
            send_sem=in_send.at[peer], recv_sem=in_recv.at[slot],
            device_id=where(peer), device_id_type=MESH)

    def extra_copy(peer, slot):
        return pltpu.make_async_remote_copy(
            src_ref=extra, dst_ref=extra_all.at[slot],
            send_sem=ex_send.at[peer], recv_sem=ex_recv.at[slot],
            device_id=where(peer), device_id_type=MESH)

    def result_copy(peer, slot):
        return pltpu.make_async_remote_copy(
            src_ref=outbox.at[peer], dst_ref=out.at[slot],
            send_sem=out_send.at[peer], recv_sem=out_recv.at[slot],
            device_id=where(peer), device_id_type=MESH)

    barrier = pltpu.get_barrier_semaphore()

    def greet(k, c):
        pl.semaphore_signal(barrier, inc=1, device_id=where(lax.rem(me + k, n)), device_id_type=MESH)
        return c

    lax.fori_loop(1, n, greet, 0)
    inbox[me] = pieces[me]
    extra_all[me] = extra[...]
    pl.semaphore_wait(barrier, n - 1)

    def send(k, c):
        peer = lax.rem(me + k, n)
        extra_copy(peer, me).start()
        piece_copy(peer, me).start()
        return c

    lax.fori_loop(1, n, send, 0)

    lane = lax.broadcasted_iota(jnp.int32, (rows, 128), 1) * head_dim
    index = lax.broadcasted_iota(jnp.int32, (rows, 128), 0) + me * rows
    mine = (index >= lane) & (index < lane + head_dim)

    def step(i, state):
        b = n - 1 - i if reverse else i

        @pl.when(b != me)
        def _():
            extra_copy(b, b).wait_recv()
            piece_copy(b, b).wait_recv()

        outbox[b] = state.astype(jnp.bfloat16)

        @pl.when(b != me)
        def _():
            result_copy(b, me).start()

        row = decays[b]
        factor = jnp.exp(jnp.sum(jnp.where(mine, row, 0.0), axis=1, keepdims=True))
        return factor * state + inbox[b].astype(jnp.float32)

    lax.fori_loop(0, n, step, jnp.zeros(inbox.shape[1:], jnp.float32))
    out[me] = outbox[me]

    def finish(k, c):
        peer = lax.rem(me + k, n)
        extra_copy(peer, peer).wait_send()
        piece_copy(peer, peer).wait_send()
        result_copy(peer, peer).wait_send()
        result_copy(peer, peer).wait_recv()
        return c

    lax.fori_loop(1, n, finish, 0)


def carried(state, extra, decays, reverse):
    n = lax.axis_size("seq")
    heads, depth, width = state.shape
    total = heads * depth
    rows = -(-total // (16 * n)) * 16
    flat = jnp.pad(state.reshape(total, width), ((0, n * rows - total), (0, 0)))
    pieces = flat.reshape(n, rows, width)
    vmem = pl.BlockSpec(memory_space=pltpu.VMEM)
    args = (pieces, extra) + ((decays,) if reverse else ())
    out, gathered = pl.pallas_call(
        functools.partial(scan_kernel, n, rows, depth, reverse),
        out_shape=(
            jax.ShapeDtypeStruct((n, rows, width), jnp.bfloat16),
            jax.ShapeDtypeStruct((n,) + extra.shape, jnp.float32),
        ),
        in_specs=[vmem] * len(args),
        out_specs=(vmem, vmem),
        scratch_shapes=[pltpu.VMEM((n, rows, width), jnp.bfloat16)] * 2
        + [pltpu.SemaphoreType.DMA((n,))] * 6,
        compiler_params=pltpu.CompilerParams(
            collective_id=1 if reverse else 0, has_side_effects=True, vmem_limit_bytes=48 << 20),
        name="adjoint_scan" if reverse else "state_scan",
    )(*args)
    return out.reshape(n * rows, width)[:total].reshape(heads, depth, width), gathered


def tail_kernel(n, terms, edge, total, following, held, landed, send_sem, recv_sem, edge_send, edge_recv):
    me = lax.axis_index("seq")
    group = lax.axis_index("groups")
    steps = n.bit_length() - 1
    barrier = pltpu.get_barrier_semaphore()
    partners = [me + (1 << i) - (2 << i) * ((me // (1 << i)) % 2) for i in range(steps)]
    for partner in partners:
        pl.semaphore_signal(barrier, inc=1, device_id=(group, partner), device_id_type=MESH)
    before, after = lax.rem(me + n - 1, n), lax.rem(me + 1, n)
    for peer in (before, after):
        pl.semaphore_signal(barrier, inc=1, device_id=(group, peer), device_id_type=MESH)
    pl.semaphore_wait(barrier, steps + 2)
    edge_copy = pltpu.make_async_remote_copy(
        src_ref=edge, dst_ref=following, send_sem=edge_send, recv_sem=edge_recv,
        device_id=(group, before), device_id_type=MESH)
    edge_copy.start()
    held[0] = terms[...]
    for i, partner in enumerate(partners):
        copy = pltpu.make_async_remote_copy(
            src_ref=held.at[i], dst_ref=landed.at[i], send_sem=send_sem.at[i], recv_sem=recv_sem.at[i],
            device_id=(group, partner), device_id_type=MESH)
        copy.start()
        copy.wait()
        held[i + 1] = held[i] + landed[i]
    total[...] = held[steps]
    edge_copy.wait()


def tail_exchange(terms, edge):
    n = lax.axis_size("seq")
    steps = n.bit_length() - 1
    vmem = pl.BlockSpec(memory_space=pltpu.VMEM)
    return pl.pallas_call(
        functools.partial(tail_kernel, n),
        out_shape=(jax.ShapeDtypeStruct(terms.shape, jnp.float32), jax.ShapeDtypeStruct(edge.shape, jnp.float32)),
        in_specs=[vmem, vmem],
        out_specs=(vmem, vmem),
        scratch_shapes=[
            pltpu.VMEM((steps + 1,) + terms.shape, jnp.float32),
            pltpu.VMEM((steps,) + terms.shape, jnp.float32),
            pltpu.SemaphoreType.DMA((steps,)),
            pltpu.SemaphoreType.DMA((steps,)),
            pltpu.SemaphoreType.DMA,
            pltpu.SemaphoreType.DMA,
        ],
        compiler_params=pltpu.CompilerParams(collective_id=2, has_side_effects=True),
        name="tail_exchange",
    )(terms, edge)


def passed_along(value, axis):
    count = lax.axis_size(axis)
    return lax.ppermute(value, axis, [(s, s + 1) for s in range(count - 1)])


def frame_layout(lengths, decays, count):
    bounds = jnp.cumsum(lengths)
    position = jnp.arange(count, dtype=jnp.int32)
    frame_id = jnp.sum((position[:, None] >= bounds[None, :]).astype(jnp.int32), axis=1)
    frame_cum = jnp.cumsum(decays, axis=0)
    frame_numbers = jnp.arange(lengths.shape[0], dtype=jnp.int32)
    selector = (frame_id[:, None] == frame_numbers[None, :]).astype(jnp.float32)
    token_decay = jnp.sum(selector[:, :, None] * frame_cum[None, :, :], axis=1)
    return (frame_id, token_decay, frame_cum)


def decay_weights(frame_id, token_decay):
    allowed = (frame_id[:, None] >= frame_id[None, :])[None, :, :]
    head_major = token_decay.T
    spread = head_major[:, :, None] - head_major[:, None, :]
    return jnp.where(allowed, jnp.exp(jnp.where(allowed, spread, 0.0)), 0.0)


def causal_conv(padded, kernel, count):
    tap_count = kernel.shape[0]
    computed_output = jnp.zeros((count, kernel.shape[1]), jnp.float32)
    for offset in range(tap_count):
        computed_output = (
            computed_output
            + kernel[offset] * padded[tap_count - 1 - offset : tap_count - 1 - offset + count]
        )
    return computed_output


def conv_back(padded_grad, kernel, count):
    computed_output = jnp.zeros((count, kernel.shape[1]), jnp.float32)
    for offset in range(kernel.shape[0]):
        computed_output = computed_output + kernel[offset] * padded_grad[offset : offset + count]
    return computed_output


def framed_outer(left, right, frame_id, weights):
    result = 0.0
    for f in range(weights.shape[0]):
        part = jnp.where((frame_id == f)[:, None, None], left, jnp.zeros_like(left))
        result = result + weights[f][:, None, None] * jnp.einsum(
            "thd,the->hde", part, right, preferred_element_type=jnp.float32)
    return result.astype(jnp.bfloat16)


def body(
    queries,
    key_rows,
    value_rows,
    frame_len,
    log_decay,
    timestep,
    conv_kernel,
    norm_gain,
    mod_table,
    out_grad,
):
    f32 = jnp.float32
    row_count, channels = queries.shape
    head_count = log_decay.shape[2]
    head_dim = channels // head_count
    score_scale = head_dim ** (-0.5)
    tap_count = conv_kernel.shape[0]
    block_count = lax.axis_size("seq")
    place = lax.axis_index("seq")
    frame_id, token_decay, frame_cum = frame_layout(frame_len[0], log_decay[0], row_count)
    block_decay = frame_cum[-1]
    previous = passed_along(value_rows[row_count - (tap_count - 1) :], "seq")
    padded = jnp.concatenate([previous, value_rows], axis=0).astype(f32)
    conv_values = causal_conv(padded, conv_kernel, row_count).astype(jnp.bfloat16)
    query_heads = queries.reshape(row_count, head_count, head_dim)
    key_heads = key_rows.reshape(row_count, head_count, head_dim)
    value_heads = conv_values.reshape(row_count, head_count, head_dim)
    into_end = jnp.exp(block_decay[None, :] - token_decay)
    from_start = jnp.exp(token_decay)
    local_state = framed_outer(key_heads, value_heads, frame_id, jnp.exp(block_decay[None, :] - frame_cum))
    lanes = jnp.concatenate([
        block_decay, timestep.astype(f32), jnp.zeros((128 - head_count - 1,), f32)])[None, :]
    state_in, gathered = carried(local_state, lanes, None, False)
    weights_mask = decay_weights(frame_id, token_decay)
    scores = jnp.einsum("thd,shd->hts", query_heads, key_heads, preferred_element_type=f32)
    attn_weights = (scores * weights_mask * score_scale).astype(jnp.bfloat16)
    numerator = jnp.einsum("hts,shd->thd", attn_weights, value_heads, preferred_element_type=f32)
    row_scale = (score_scale * from_start)[:, :, None]
    numerator = numerator + row_scale * jnp.einsum(
        "thd,hde->the", query_heads, state_in, preferred_element_type=f32)
    inv_rms = lax.rsqrt(jnp.mean(numerator * numerator, axis=2, keepdims=True) + EPSILON)
    normed = numerator * inv_rms
    levels = jnp.arange(mod_table.shape[0], dtype=jnp.int32)
    selector = (timestep[0] == levels).astype(f32)
    mod_row = jnp.sum(selector[:, None] * mod_table, axis=0)
    upstream = out_grad.astype(f32).reshape(row_count, head_count, head_dim)
    normed_grad = upstream * (norm_gain * (1.0 + mod_row)).reshape(head_count, head_dim)
    numer_grad = inv_rms * (
        normed_grad - normed * jnp.mean(normed_grad * normed, axis=2, keepdims=True)
    )
    grad_rounded = numer_grad.astype(jnp.bfloat16)
    block_terms = jnp.sum((upstream * normed).reshape(row_count, channels), axis=0)
    adjoint_local = framed_outer(query_heads, grad_rounded, frame_id, score_scale * jnp.exp(frame_cum))
    adjoint, terms_all = carried(adjoint_local, block_terms[None, :], gathered, True)
    score_grad = jnp.einsum("thd,shd->hts", grad_rounded, value_heads, preferred_element_type=f32)
    score_grad = (score_grad * weights_mask * score_scale).astype(jnp.bfloat16)
    query_grad = jnp.einsum("hts,shd->thd", score_grad, key_heads, preferred_element_type=f32)
    query_grad = query_grad + row_scale * jnp.einsum(
        "the,hde->thd", grad_rounded, state_in, preferred_element_type=f32)
    key_grad = jnp.einsum("hts,thd->shd", score_grad, query_heads, preferred_element_type=f32)
    key_grad = key_grad + into_end[:, :, None] * jnp.einsum(
        "the,hde->thd", value_heads, adjoint, preferred_element_type=f32)
    value_grad = jnp.einsum("hts,thd->shd", attn_weights, grad_rounded, preferred_element_type=f32)
    value_grad = value_grad + into_end[:, :, None] * jnp.einsum(
        "thd,hde->the", key_heads, adjoint, preferred_element_type=f32)
    conv_grad = value_grad.reshape(row_count, channels)
    kernel_terms = jnp.stack(
        [
            jnp.sum(
                conv_grad * padded[tap_count - 1 - offset : tap_count - 1 - offset + row_count],
                axis=0,
            )
            for offset in range(tap_count)
        ],
        axis=0,
    )
    kernel_sum, following = tail_exchange(kernel_terms, conv_grad[: tap_count - 1])
    following = jnp.where(place == block_count - 1, 0.0, following)
    padded_grad = jnp.concatenate([conv_grad, following], axis=0)
    input_grad = conv_back(padded_grad, conv_kernel, row_count)
    terms = terms_all[:, 0, :]
    chosen = (gathered[:, 0, head_count].astype(jnp.int32)[:, None] == levels[None, :]).astype(f32)
    sums = jnp.einsum("bl,bc->lc", chosen, terms, precision=lax.Precision.HIGHEST)
    gain_sum = jnp.sum(sums * (1.0 + mod_table), axis=0)
    table_sum = sums * norm_gain
    return (
        query_grad.reshape(row_count, channels).astype(jnp.bfloat16),
        key_grad.reshape(row_count, channels).astype(jnp.bfloat16),
        input_grad.astype(jnp.bfloat16),
        kernel_sum / block_count,
        gain_sum / block_count,
        table_sum / block_count,
    )


def solution(mesh):
    in_specs = (
        P(("groups", "seq"), None),
        P(("groups", "seq"), None),
        P(("groups", "seq"), None),
        P(("groups", "seq"), None),
        P(("groups", "seq"), None, None),
        P(("groups", "seq")),
        P(),
        P(),
        P(),
        P(("groups", "seq"), None),
    )
    out_specs = (
        P(("groups", "seq"), None),
        P(("groups", "seq"), None),
        P(("groups", "seq"), None),
        P("groups", None),
        P("groups"),
        P("groups", None),
    )
    return jax.shard_map(body, mesh=mesh, in_specs=in_specs, out_specs=out_specs, check_vma=False)
```

time: 520 us -> 177 us (0.34); the launches traced: 512 us -> 176 us
  waiting for transfers between devices: 252 us -> 0.01 us
  Pallas kernels: 0 us -> 86.4 us
  blocking collectives: 81.3 us -> 0 us
  other arithmetic: 76.3 us -> 39.2 us
  matrix products: 58.6 us -> 38.7 us
  local copies, waits for them, and re-layouts: 24.1 us -> 7.97 us
  between operations: 15.5 us -> 1.76 us
    all_gather x2 -> x0, waiting for transfers between devices: 165 us -> none  [carried_in(): gathered = jax.tree.map(lambda a: lax.all_gather(a, axis), part)]
    psum x1 -> x0, waiting for transfers between devices: 87.6 us -> none  [body(): lax.psum((gain_terms, kernel_terms, table_local), 'seq')]
    pallas_call x0 -> x3, Pallas kernels: none -> 86.4 us  [the longest x2 72.3 us: carried(): pl.pallas_call(functools.partial(scan_kernel, n, rows, depth, reverse), o...]
    psum x1 -> x0, blocking collectives: 58.7 us -> none  [body(): lax.psum((gain_terms, kernel_terms, table_local), 'seq')]
    add x15 -> x0, other arithmetic: 41.7 us -> none  [combine_maps(): later[0][:, None, None] * earlier[1] + later[1]]
    all_gather x1 -> x0, blocking collectives: 22.6 us -> none  [carried_in(): gathered = jax.tree.map(lambda a: lax.all_gather(a, axis), part)]
    dot_general x6 -> x9, matrix products: 29.9 us -> 11.7 us  [the longest x4 3.07 us: framed_outer(): jnp.einsum('thd,the->hde', part, right, preferred_element_type=jnp.float32)]
    convert_element_type x2 -> x5, other arithmetic: 1.05 us -> 14.4 us  [the longest x1 11.9 us: body(): input_grad.astype(jnp.bfloat16)]
  transfers between devices with their start and end apart: 5 -> 1, of which waited for: 3 -> 0; matrix products, arithmetic and copies ran while one was open for 8% -> 7% of each run, Pallas kernels for 0% -> 0%
where the time goes in v1:
time: 177 us; the launch traced here: 176 us
  Pallas kernels  86.4 us (49%)
  other arithmetic  39.2 us (22%)
  matrix products  38.7 us (22%)
  local copies, waits for them, and re-layouts  7.97 us (5%)
  starting transfers between devices  2.36 us (1%)
    pallas_call x2, Pallas kernels, carried(): pl.pallas_call(functools.partial(scan_kernel, n, rows, depth, reverse), o...  72.3 us
    pallas_call x1, Pallas kernels, tail_exchange(): pl.pallas_call(functools.partial(tail_kernel, n), out_shape=(jax.ShapeDty...  14.1 us
    reduce_sum x1, other arithmetic, body(): jnp.sum(conv_grad * padded[tap_count - 1 - offset:tap_count - 1 - offset...  12.2 us
    convert_element_type x1, other arithmetic, body(): input_grad.astype(jnp.bfloat16)  11.9 us
    dot_general x1, matrix products, body(): jnp.einsum('thd,shd->hts', query_heads, key_heads, preferred_element_type...  7.5 us
    dot_general x1, matrix products, body(): jnp.einsum('thd,shd->hts', grad_rounded, value_heads, preferred_element_t...  5.93 us
    convert_element_type x1, other arithmetic, body(): causal_conv(padded, conv_kernel, row_count).astype(jnp.bfloat16)  4.29 us
    dot_general x1, matrix products, body(): jnp.einsum('hts,thd->shd', score_grad, query_heads, preferred_element_typ...  4.24 us
  transfers between devices with their start and end apart: 1, of which 0 were waited for; matrix products, arithmetic and copies ran while one was open for 7% of the time, Pallas kernels for 0%

profile of v1, /device:TPU:0, one launch (start us, length us, event | category | flops | bytes accessed | tf_op | source)
XLA Modules:
  0.0 176.4 jit_solution(11324709684664918683)
XLA Ops:
  0.6 1.3 slice.75
  2.2 2.4 %collective-permute-start = (bf16[3,2240]{1,0:T(4,128)(2,1)S(1)}, bf16[3,2240]{1,0:T(4,128)(2,1)S(1)}, u32[]{:S(2)}, u32[]{:S(2)}) collective-permute-start(bf16[3,2240]{1,0:T(4,128)(2,1)S(1)} %copy.41), channel_id=1, source_target_pairs={{0,1},{1,2},{2,3},{3,4},{4,5},{5,6},{6,7},{7,8},{8,9},{9,10},{10,1... | collective-permute-start | bytes 40328 | tf_op jit(solution)/shard_map/ppermute | solution.py:178
  5.3 0.8 reduce-window.8
  6.4 1.0 slice_reduce_fusion.3
  8.4 1.2 multiply_reduce_fusion.6
  9.6 0.7 add_multiply_fusion
  10.3 7.5 %multiply_convert_fusion.1 = bf16[20,384,384]{2,1,0:T(8,128)(2,1)} fusion(f32[20,384]{1,0:T(8,128)S(1)} %bitcast.128, pred[384,384]{1,0:T(8,128)(4,1)S(1)} %broadcast_compare_fusion, bf16[384,20,112]{0,2,1:T(8,128)(2,1)} %bitcast.107, bf16[384,20,112]{0,2,1:T(8,128)(2,1)} %bitcast.114), kind=kOutput, calls=%fused_computation.1 | convolution fusion | flops 678297600 | bytes 9517056 | tf_op jit(solution)/shard_map/thd,shd->hts/dot_general | solution.py:261
  18.3 1.1 maximum_convert_fusion
  19.4 4.3 %add_convert_fusion = bf16[384,2240]{0,1:T(8,128)(2,1)S(1)} fusion(f32[387,2240]{0,1:T(8,128)S(1)} %maximum_convert_fusion, f32[2240]{0:T(1024)S(1)} %get-tuple-element.26, f32[2240]{0:T(1024)S(1)} %get-tuple-element.27, f32[2240]{0:T(1024)S(1)} %get-tuple-element.25, f32[2240]{0:T(1024)S(1)} %get-tuple-element.24), kind=kLoop, calls=%fused_computation.40 | loop fusion | flops 6881280 | bytes 15518720 | tf_op jit(solution)/shard_map/convert_element_type | solution.py:250
  23.7 0.7 fusion.39
  24.5 0.8 fusion.54
  25.4 29.0 %state_scan.1 = (bf16[16,144,112]{2,1,0:T(8,128)(2,1)S(1)}, f32[16,1,128]{2,1,0:T(1,128)S(1)}) custom-call(bf16[16,144,112]{2,1,0:T(8,128)(2,1)S(1)} %bitcast.93, f32[1,128]{1,0:T(1,128)S(1)} %maximum_bitcast_fusion.refs_1_), custom_call_target="tpu_custom_call" | custom-call | tf_op jit(solution)/shard_map/state_scan/pallas_call | solution.py:109
  55.2 2.0 %multiply_reduce_fusion.4 = (f32[384,20]{0,1:T(8,128)S(1)}, f32[384,20,112]{0,2,1:T(8,128)S(1)}) fusion(f32[20,112,384]{2,1,0:T(8,128)S(1)} %fusion.70, f32[384,20]{0,1:T(8,128)S(1)} %get-tuple-element.31, bf16[384,20,112]{0,2,1:T(8,128)(2,1)S(1)} %bitcast.104, bf16[20,384,384]{2,1,0:T(8,128)(2,1)S(1)} %bitcast.101), kind=kOutput, calls=%fused_computation.39 | convolution fusion | flops 664035840 | bytes 14561280 | tf_op jit(solution)/shard_map/hts,shd->thd/dot_general | solution.py:263
  57.2 1.6 fusion.5
  58.9 1.0 fusion.4
  59.9 5.9 %multiply_convert_fusion = bf16[20,384,384]{2,1,0:T(8,128)(2,1)} fusion(f32[20,384]{1,0:T(8,128)S(1)} %bitcast.129, pred[384,384]{1,0:T(8,128)(4,1)S(1)} %broadcast_compare_fusion, bf16[384,20,112]{0,2,1:T(8,128)(2,1)S(1)} %fusion.4, bf16[384,20,112]{0,2,1:T(8,128)(2,1)S(1)} %bitcast.105), kind=kOutput, calls=%fused_computation | convolution fusion | flops 678297600 | bytes 9517056 | tf_op jit(solution)/shard_map/thd,shd->hts/dot_general | solution.py:281
  65.9 2.5 %fusion.71 = f32[20,112,384]{2,1,0:T(8,128)} fusion(bf16[20,112,112]{2,1,0:T(8,128)(2,1)S(1)} %bitcast.122, bf16[384,20,112]{0,2,1:T(8,128)(2,1)S(1)} %fusion.4), kind=kOutput, calls=%fused_computation.109 | convolution fusion | flops 192675840 | bytes 5662720 | tf_op jit(solution)/shard_map/the,hde->thd/dot_general | solution.py:284
  68.4 0.8 fusion.48
  69.1 0.8 fusion.51
  70.6 43.3 %adjoint_scan.1 = (bf16[16,144,112]{2,1,0:T(8,128)(2,1)S(1)}, f32[16,1,2240]{2,1,0:T(1,128)S(1)}) custom-call(bf16[16,144,112]{2,1,0:T(8,128)(2,1)S(1)} %bitcast.92, f32[1,2240]{1,0:T(1,128)S(1)} %broadcast_in_dim.78.refs_1_, f32[16,1,128]{2,1,0:T(1,128)S(1)} %get-tuple-element.13.refs_2_), custom_call_target="tpu_custom_call" | custom-call | tf_op jit(solution)/shard_map/adjoint_scan/pallas_call | solution.py:109
  113.9 2.1 %fusion.72 = f32[20,112,384]{2,1,0:T(8,128)S(1)} fusion(bf16[20,112,112]{2,1,0:T(8,128)(2,1)S(1)} %bitcast.119, bf16[384,20,112]{0,2,1:T(8,128)(2,1)} %bitcast.115), kind=kOutput, calls=%fused_computation.110 | convolution fusion | flops 192675840 | bytes 5662720 | tf_op jit(solution)/shard_map/thd,hde->the/dot_general | solution.py:290
  116.1 4.1 %fusion.15 = f32[384,20,112]{0,2,1:T(8,128)S(1)} fusion(f32[20,112,384]{2,1,0:T(8,128)S(1)} %fusion.72, bf16[384,20,112]{0,2,1:T(8,128)(2,1)S(1)} %fusion.4, bf16[20,384,384]{2,1,0:T(8,128)(2,1)} %multiply_convert_fusion.1, f32[384,20]{0,1:T(8,128)S(1)} %get-tuple-element.30), kind=kOutput, calls=%fused_computation.26 | convolution fusion | flops 662323200 | bytes 14530560 | tf_op jit(solution)/shard_map/hts,thd->shd/dot_general | solution.py:289
  120.2 1.8 %copy-done.1 = f32[384,20,112]{0,2,1:T(8,128)} copy-done((f32[384,20,112]{0,2,1:T(8,128)}, f32[384,20,112]{0,2,1:T(8,128)S(1)}, u32[]{:S(2)}) %copy-start.1) | copy-done | bytes 3440664
  122.0 1.0 copy.39.edge
  123.0 12.2 %multiply_reduce_fusion.3 = (f32[2240]{0:T(1024)S(1)}, f32[2240]{0:T(1024)S(1)}, f32[2240]{0:T(1024)S(1)}, f32[2240]{0:T(1024)S(1)}) fusion(f32[384,2240]{0,1:T(8,128)} %bitcast.98, f32[387,2240]{0,1:T(8,128)} %copy-done), kind=kLoop, calls=%fused_computation.38 | loop fusion | flops 6872320 | bytes 17239040 | tf_op jit(solution)/shard_map/reduce_sum | solution.py:295
  135.9 14.1 %tail_exchange.1 = (f32[4,2240]{1,0:T(4,128)}, f32[3,2240]{1,0:T(4,128)}) custom-call(f32[4,2240]{1,0:T(4,128)} %pad_maximum_fusion.1.terms, f32[3,2240]{1,0:T(4,128)} %copy.39.edge), custom_call_target="tpu_custom_call" | custom-call | tf_op jit(solution)/shard_map/tail_exchange/pallas_call | solution.py:158
  150.1 0.8 broadcast_select_fusion
  151.3 11.9 %fusion.10 = bf16[384,2240]{0,1:T(8,128)(2,1)} fusion(f32[384,2240]{0,1:T(8,128)} %bitcast.99, f32[3,2240]{0,1:T(8,128)S(1)} %copy.36, f32[2240]{0:T(1024)S(1)} %get-tuple-element.26, f32[2240]{0:T(1024)S(1)} %get-tuple-element.27, f32[2240]{0:T(1024)S(1)} %get-tuple-element.25, f32[2240]{0:T(1024)S(1)} %get-tuple-element.24), kind=kLoop, calls=%fused_computation.19 | loop fusion | flops 9461760 | bytes 5223680 | tf_op jit(solution)/shard_map/convert_element_type | solution.py:315
  163.2 1.4 multiply_multiply_fusion
  165.8 4.2 %fusion.73 = f32[20,384,112]{1,2,0:T(8,128)S(1)} fusion(bf16[384,20,112]{0,2,1:T(8,128)(2,1)S(1)} %bitcast.111, bf16[20,384,384]{2,1,0:T(8,128)(2,1)} %multiply_convert_fusion), kind=kOutput, calls=%fused_computation.111 | convolution fusion | flops 660602880 | bytes 11059200 | tf_op jit(solution)/shard_map/hts,thd->shd/dot_general | solution.py:286
  170.1 2.0 %fusion.17 = bf16[384,20,112]{0,2,1:T(8,128)(2,1)} fusion(f32[20,384,112]{1,2,0:T(8,128)S(1)} %fusion.73, bf16[20,112,112]{2,1,0:T(8,128)(2,1)S(1)} %bitcast.120, bf16[384,20,112]{0,2,1:T(8,128)(2,1)S(1)} %bitcast.106, f32[384,20]{0,1:T(8,128)S(1)} %get-tuple-element.30), kind=kOutput, calls=%fused_computation.29 | convolution fusion | flops 195256320 | bytes 7413760 | tf_op jit(solution)/shard_map/the,hde->thd/dot_general | solution.py:287
  173.2 3.2 %fusion.19 = bf16[384,20,112]{0,2,1:T(8,128)(2,1)} fusion(f32[20,112,384]{2,1,0:T(8,128)S(1)} %copy-done.6, bf16[20,384,384]{2,1,0:T(8,128)(2,1)S(1)} %bitcast.97, bf16[384,20,112]{0,2,1:T(8,128)(2,1)S(1)} %bitcast.118, f32[384,20]{0,1:T(8,128)S(1)} %get-tuple-element.31), kind=kOutput, calls=%fused_computation.32 | convolution fusion | flops 663183360 | bytes 12810240 | tf_op jit(solution)/shard_map/hts,shd->thd/dot_general | solution.py:283
  (73 shorter events, 7.2 us)
Async XLA Ops:
  2.2 15.8 %collective-permute-start = (bf16[3,2240]{1,0:T(4,128)(2,1)S(1)}, bf16[3,2240]{1,0:T(4,128)(2,1)S(1)}, u32[]{:S(2)}, u32[]{:S(2)}) collective-permute-start(bf16[3,2240]{1,0:T(4,128)(2,1)S(1)} %copy.41), channel_id=1, source_target_pairs={{0,1},{1,2},{2,3},{3,4},{4,5},{5,6},{6,7},{7,8},{8,9},{9,10},{10,1... | collective-permute-start | bytes 40328 | tf_op jit(solution)/shard_map/ppermute | solution.py:178
  10.3 8.0 %copy-start.10 = (bf16[384,2240]{0,1:T(8,128)(2,1)S(1)}, bf16[384,2240]{0,1:T(8,128)(2,1)}, u32[]{:S(2)}) copy-start(bf16[384,2240]{0,1:T(8,128)(2,1)} %param.12) | copy-start | bytes 5160964
  19.4 4.3 %copy-start = (f32[387,2240]{0,1:T(8,128)}, f32[387,2240]{0,1:T(8,128)S(1)}, u32[]{:S(2)}) copy-start(f32[387,2240]{0,1:T(8,128)S(1)} %maximum_convert_fusion) | copy-start | bytes 10402564
  19.4 4.3 %copy-start.8 = (bf16[384,2240]{0,1:T(8,128)(2,1)S(1)}, bf16[384,2240]{0,1:T(8,128)(2,1)}, u32[]{:S(2)}) copy-start(bf16[384,2240]{0,1:T(8,128)(2,1)} %param.11) | copy-start | bytes 5160964
  23.7 36.2 %copy-start.2 = (bf16[384,2240]{0,1:T(8,128)(2,1)}, bf16[384,2240]{0,1:T(8,128)(2,1)S(1)}, u32[]{:S(2)}) copy-start(bf16[384,2240]{0,1:T(8,128)(2,1)S(1)} %add_convert_fusion) | copy-start | bytes 5160964
  23.7 31.4 %slice-start.2 = ((s8[5898240]{0:T(1024)(128)(4,1)}), s8[4194304]{0:T(1024)(128)(4,1)S(1)}, s32[]{:S(2)}) async-start(s8[5898240]{0:T(1024)(128)(4,1)} %bitcast.100), calls=%async_computation.2 | async-start | bytes 8388608
  24.5 30.0 %copy-start.4 = (bf16[384,2240]{0,1:T(8,128)(2,1)S(1)}, bf16[384,2240]{0,1:T(8,128)(2,1)}, u32[]{:S(2)}) copy-start(bf16[384,2240]{0,1:T(8,128)(2,1)} %param.10) | copy-start | bytes 5160964
  24.5 30.7 %slice-start.3 = ((s8[5898240]{0:T(1024)(128)(4,1)}), s8[1703936]{0:T(1024)(128)(4,1)S(1)}, s32[]{:S(2)}) async-start(s8[5898240]{0:T(1024)(128)(4,1)} %bitcast.100), calls=%async_computation.3 | async-start | bytes 3407872
  55.2 2.1 %copy-start.7 = (bf16[384,2240]{0,1:T(8,128)(2,1)S(1)}, bf16[384,2240]{0,1:T(8,128)(2,1)}, u32[]{:S(2)}) copy-start(bf16[384,2240]{0,1:T(8,128)(2,1)} %param.19) | copy-start | bytes 5160964
  120.2 1.8 %copy-start.1 = (f32[384,20,112]{0,2,1:T(8,128)}, f32[384,20,112]{0,2,1:T(8,128)S(1)}, u32[]{:S(2)}) copy-start(f32[384,20,112]{0,2,1:T(8,128)S(1)} %fusion.15) | copy-start | bytes 10321924
  151.3 11.9 %copy-start.11 = (f32[50,2240]{1,0:T(8,128)S(1)}, f32[50,2240]{1,0:T(8,128)}, u32[]{:S(2)}) copy-start(f32[50,2240]{1,0:T(8,128)} %param.18) | copy-start | bytes 1344004
  151.3 11.9 %copy-start.12 = (f32[2240]{0:T(1024)S(1)}, f32[2240]{0:T(1024)}, u32[]{:S(2)}) copy-start(f32[2240]{0:T(1024)} %param.17) | copy-start | bytes 26884
  151.3 13.9 %copy-start.13 = (f32[4,2240]{1,0:T(4,128)S(1)}, f32[4,2240]{1,0:T(4,128)}, u32[]{:S(2)}) copy-start(f32[4,2240]{1,0:T(4,128)} %get-tuple-element.16) | copy-start | bytes 107524
  151.3 14.5 %copy-start.5 = (bf16[384,2240]{0,1:T(8,128)(2,1)S(1)}, bf16[384,2240]{0,1:T(8,128)(2,1)}, u32[]{:S(2)}) copy-start(bf16[384,2240]{0,1:T(8,128)(2,1)} %param.10) | copy-start | bytes 5160964
  163.2 8.9 %slice-start = ((s8[5898240]{0:T(1024)(128)(4,1)}), s8[4194304]{0:T(1024)(128)(4,1)S(1)}, s32[]{:S(2)}) async-start(s8[5898240]{0:T(1024)(128)(4,1)} %bitcast.96), calls=%async_computation | async-start | bytes 8388608
  165.8 4.2 %copy-start.3 = (bf16[384,2240]{0,1:T(8,128)(2,1)S(1)}, bf16[384,2240]{0,1:T(8,128)(2,1)}, u32[]{:S(2)}) copy-start(bf16[384,2240]{0,1:T(8,128)(2,1)} %copy-done.2) | copy-start | bytes 5160964
  165.8 6.2 %slice-start.1 = ((s8[5898240]{0:T(1024)(128)(4,1)}), s8[1703936]{0:T(1024)(128)(4,1)S(1)}, s32[]{:S(2)}) async-start(s8[5898240]{0:T(1024)(128)(4,1)} %bitcast.96), calls=%async_computation.1 | async-start | bytes 3407872
  170.0 2.5 %copy-start.6 = (f32[20,112,384]{2,1,0:T(8,128)S(1)}, f32[20,112,384]{2,1,0:T(8,128)}, u32[]{:S(2)}) copy-start(f32[20,112,384]{2,1,0:T(8,128)} %fusion.71) | copy-start | bytes 10321924
  170.1 3.1 %copy-start.9 = (bf16[384,2240]{0,1:T(8,128)(2,1)S(1)}, bf16[384,2240]{0,1:T(8,128)(2,1)}, u32[]{:S(2)}) copy-start(bf16[384,2240]{0,1:T(8,128)(2,1)} %param.11) | copy-start | bytes 5160964
